TPU v7x, 128 devices: a whole 4x4x4 slice. The times are simulated.
128 devices in a mesh: ctx: 32 (over z, y, x_lo), head: 4 (over x_hi, core).
Axes of the slice: x: 4 (x_hi: 2, x_lo: 2; x = x_hi * 2 + x_lo), y: 4, z: 4, core: 2. Of those that a mesh axis runs over, the one named last changes fastest.
Arguments:
- tokens: bfloat16 [12288, 4096], P('ctx', 'head'), may hold values from -6 to 6
- doc_ids: int32 [12288], replicated, may hold values from 0 to 3, never falling along the last dimension, each value on 1 to 9216 neighbouring positions
- norm_gain: float32 [4096], replicated, may hold values from 0.25 to 1.75
- w_query: bfloat16 [4096, 4096], P(None, 'head'), may hold values from -4 to 4
- w_key: bfloat16 [4096, 1024], P(None, 'head'), may hold values from -0.09375 to 0.09375
- w_value: bfloat16 [4096, 1024], P(None, 'head'), may hold values from -0.09375 to 0.09375
- w_out: bfloat16 [4096, 4096], P('head'), may hold values from -0.09375 to 0.09375
Outputs:
- layer_out: bfloat16 [12288, 4096], P('ctx', 'head')
Inputs may be any that keep to these rules, and one draw needn't show every extreme that they name: `doc_ids`: never falling along the sequence; 4 documents, one of exactly 9216 tokens.
All inputs are finite; a program needn't handle non-finite values.
Results may differ from a plain program's by a relative error of at most 0.012.
The roundings to bfloat16 on the way count: a program that leaves them out, or rounds other values in their place, can miss the bound.
Values may be sent and summed in bfloat16 or wider, within the bound.
A program may use at most 128 MiB of HBM per device.

v0:
```python
import math

import jax
import jax.numpy as jnp
from jax import lax
from jax.sharding import PartitionSpec as P

HD = 128


THETA = 500000.0
SENTINEL = -1e30


def rotate(values, positions):
    head_width = values.shape[-1]
    midpoint = head_width // 2
    exponents = jnp.arange(midpoint, dtype=jnp.float32) * (2.0 / head_width)
    inverse = jnp.power(jnp.float32(THETA), -exponents)
    angles = positions.astype(jnp.float32)[:, None] * inverse[None, :]
    cosine = jnp.cos(angles)[:, None, :]
    sine_wave = jnp.sin(angles)[:, None, :]
    lower_half = values[..., :midpoint]
    upper_half = values[..., midpoint:]
    return jnp.concatenate(
        [
            lower_half * cosine - upper_half * sine_wave,
            upper_half * cosine + lower_half * sine_wave,
        ],
        axis=-1,
    )


def on_device(tokens, doc_ids, norm_gain, w_query, w_key, w_value, w_out):
    row_count = tokens.shape[0]
    ctx_index = lax.axis_index("ctx")
    positions = ctx_index * row_count + jnp.arange(row_count, dtype=jnp.int32)
    full_rows = lax.all_gather(tokens, "head", axis=1, tiled=True)
    floats = full_rows.astype(jnp.float32)
    spread = jnp.mean(floats * floats, axis=-1, keepdims=True)
    normed = (floats * lax.rsqrt(spread + 1e-05) * norm_gain[None, :]).astype(jnp.bfloat16)
    query_count = w_query.shape[1] // HD
    kv_count = w_key.shape[1] // HD
    group_size = query_count // kv_count
    queries = jnp.dot(normed, w_query, preferred_element_type=jnp.float32).reshape(
        row_count, query_count, HD
    )
    queries = rotate(queries, positions).astype(jnp.bfloat16)
    queries = queries.reshape(row_count, kv_count, group_size, HD).transpose(1, 2, 0, 3)
    keys_local = jnp.dot(normed, w_key, preferred_element_type=jnp.float32).reshape(
        row_count, kv_count, HD
    )
    keys_local = (
        rotate(keys_local, positions).astype(jnp.bfloat16).reshape(row_count, kv_count * HD)
    )
    values_local = jnp.dot(normed, w_value, preferred_element_type=jnp.float32).astype(jnp.bfloat16)
    starts = jnp.searchsorted(doc_ids, doc_ids[positions], side="left")
    query_block = math.gcd(row_count, 256)
    query_tiles = row_count // query_block
    score_scale = HD ** (-0.5)
    zero_high = jnp.full((kv_count, group_size, row_count), SENTINEL, jnp.float32)
    zero_denom = jnp.zeros((kv_count, group_size, row_count), jnp.float32)
    zero_sums = jnp.zeros((kv_count, group_size, row_count, HD), jnp.float32)
    key_piece = lax.all_gather(keys_local, "ctx", axis=0, tiled=True)
    value_piece = lax.all_gather(values_local, "ctx", axis=0, tiled=True)
    piece_rows = key_piece.shape[0]
    key_block = math.gcd(piece_rows, 256)
    key_tiles = piece_rows // key_block
    piece_positions = jnp.arange(piece_rows, dtype=jnp.int32)

    def visit_tile(tile_index, partial_value):
        query_tile = tile_index // key_tiles
        key_tile = tile_index % key_tiles
        query_start = query_tile * query_block
        key_start = key_tile * key_block
        tile_positions = lax.dynamic_slice_in_dim(positions, query_start, query_block, 0)
        tile_starts = lax.dynamic_slice_in_dim(starts, query_start, query_block, 0)
        key_spots = lax.dynamic_slice_in_dim(piece_positions, key_start, key_block, 0)
        needed = (jnp.min(key_spots) <= jnp.max(tile_positions)) & (
            jnp.max(key_spots) >= jnp.min(tile_starts)
        )

        def update(partial_value):
            highest, denominator, summed = partial_value
            tile_queries = lax.dynamic_slice_in_dim(queries, query_start, query_block, 2)
            tile_keys = lax.dynamic_slice_in_dim(key_piece, key_start, key_block, 0).reshape(
                key_block, kv_count, HD
            )
            tile_values = lax.dynamic_slice_in_dim(value_piece, key_start, key_block, 0).reshape(
                key_block, kv_count, HD
            )
            scores = (
                jnp.einsum(
                    "kgqd,jkd->kgqj", tile_queries, tile_keys, preferred_element_type=jnp.float32
                )
                * score_scale
            )
            allowed = (key_spots[None, :] <= tile_positions[:, None]) & (
                key_spots[None, :] >= tile_starts[:, None]
            )
            scores = jnp.where(allowed, scores, SENTINEL)
            old_high = lax.dynamic_slice_in_dim(highest, query_start, query_block, 2)
            new_high = jnp.maximum(old_high, jnp.max(scores, axis=-1))
            weights = jnp.where(allowed, jnp.exp(scores - new_high[..., None]), 0.0)
            factor = jnp.exp(old_high - new_high)
            old_denom = lax.dynamic_slice_in_dim(denominator, query_start, query_block, 2)
            new_denom = old_denom * factor + jnp.sum(weights, axis=-1)
            old_summed = lax.dynamic_slice_in_dim(summed, query_start, query_block, 2)
            new_summed = old_summed * factor[..., None] + jnp.einsum(
                "kgqj,jkd->kgqd",
                weights.astype(jnp.bfloat16),
                tile_values,
                preferred_element_type=jnp.float32,
            )
            return (
                lax.dynamic_update_slice_in_dim(highest, new_high, query_start, 2),
                lax.dynamic_update_slice_in_dim(denominator, new_denom, query_start, 2),
                lax.dynamic_update_slice_in_dim(summed, new_summed, query_start, 2),
            )

        def keep_state(partial_value):
            return partial_value

        return lax.cond(needed, update, keep_state, partial_value)

    highest, denominator, summed = lax.fori_loop(
        0, query_tiles * key_tiles, visit_tile, (zero_high, zero_denom, zero_sums)
    )
    attended = (
        (summed / denominator[..., None])
        .transpose(2, 0, 1, 3)
        .reshape(row_count, query_count * HD)
        .astype(jnp.bfloat16)
    )
    products = jnp.dot(attended, w_out, preferred_element_type=jnp.float32)
    shares = lax.psum_scatter(
        products.astype(jnp.bfloat16), "head", scatter_dimension=1, tiled=True
    ).astype(jnp.float32)
    result = (shares + tokens.astype(jnp.float32)).astype(jnp.bfloat16)
    return result


def solution(mesh):
    in_specs = (
        P("ctx", "head"),
        P(),
        P(),
        P(None, "head"),
        P(None, "head"),
        P(None, "head"),
        P("head", None),
    )
    out_specs = P("ctx", "head")
    return jax.shard_map(
        on_device, mesh=mesh, in_specs=in_specs, out_specs=out_specs, check_vma=False
    )
```

profile of v0, /device:TPU:24, one launch (start us, length us, event | category | flops | bytes accessed | tf_op | source)
XLA Modules:
  0.0 1858.4 jit_solution(17650654648763100020)
XLA Ops:
  7.3 36.4 %all-gather.4.cloned.1.call-done = bf16[384,4096]{1,0:T(8,128)(2,1)} async-done(((bf16[384,1024]{1,0:T(8,128)(2,1)}), bf16[384,4096]{1,0:T(8,128)(2,1)}) %all-gather.4.cloned.1.call-update) | async-done | bytes 3145744 | tf_op jit(solution)/shard_map/all_gather | solution.py:38
  51.7 4.0 fusion.16
  56.7 36.9 %while.44 = (s32[]{:T(128)}, u32[384]{0:T(512)S(1)}, u32[384]{0:T(512)S(1)}, s32[12288]{0:T(1024)S(1)}, s32[384]{0:T(512)S(1)}, /*index=5*/s32[]{:T(128)}, s32[]{:T(128)}, s32[]{}) while((s32[]{:T(128)}, u32[384]{0:T(512)S(1)}, u32[384]{0:T(512)S(1)}, s32[12288]{0:T(1024)S(1)}, s32[384]{0:T(512)S(1)}, /*index=5*/s32[]{:T(128)}, ...), condition=%wide.region_1.2_spmd.clone, body=%wide.region_0.0_spmd.clone.sunk | while | flops 7940 | bytes 31085 | solution.py:57
  93.6 6.9 convolution_bitcast_fusion
  102.2 108.1 %all-gather.8.cloned.1.call-done = bf16[12288,256]{1,0:T(8,128)(2,1)} async-done(((bf16[384,256]{1,0:T(8,128)(2,1)}), bf16[12288,256]{1,0:T(8,128)(2,1)}) %all-gather.8.cloned.1.call-update) | async-done | bytes 6291472 | tf_op jit(solution)/shard_map/all_gather | solution.py:65
  210.2 8.7 copy.27
  218.9 165.5 %all-gather.6.cloned.1.call-done = bf16[12288,256]{0,1:T(8,128)(2,1)} async-done(((bf16[384,256]{0,1:T(8,128)(2,1)}), bf16[12288,256]{0,1:T(8,128)(2,1)}) %all-gather.6.cloned.1.call-update) | async-done | bytes 6291472 | tf_op jit(solution)/shard_map/all_gather | solution.py:64
  385.8 721.6 %while.43 = (s32[]{:T(128)}, f32[2,4,384]{2,1,0:T(4,128)S(1)}, f32[2,4,384]{2,1,0:T(4,128)S(1)}, f32[2,4,384,128]{3,2,1,0:T(8,128)}, s32[12288]{0:T(1024)S(1)}, ...) while((s32[]{:T(128)}, f32[2,4,384]{2,1,0:T(4,128)S(1)}, ...), condition=%wide.region_12.13_spmd, body=%wide.region_3.12_spmd.sunk | while | flops 136940304 | bytes 6503074 | solution.py:126
  410.8 7.7 conditional.2
  414.9 3.6 dynamic_update_slice.8
  422.7 7.7 conditional.2
  426.8 3.6 dynamic_update_slice.8
  434.5 7.7 conditional.2
  438.6 3.6 dynamic_update_slice.8
  446.3 7.7 conditional.2
  450.5 3.6 dynamic_update_slice.8
  458.2 7.7 conditional.2
  462.3 3.6 dynamic_update_slice.8
  650.2 7.7 conditional.2
  654.3 3.6 dynamic_update_slice.8
  662.0 7.7 conditional.2
  673.8 7.7 conditional.2
  685.7 7.7 conditional.2
  697.5 7.7 conditional.2
  889.5 7.0 conditional.2
  900.6 7.1 conditional.2
  911.8 7.1 conditional.2
  923.0 7.1 conditional.2
  934.1 7.0 conditional.2
  945.3 7.0 conditional.2
  1111.9 8.5 convolution_convert_fusion
  1120.5 729.1 %reduce-scatter.2.cloned.1.call-done = bf16[384,1024]{1,0:T(8,128)(2,1)} async-done(((bf16[384,4096]{1,0:T(8,128)(2,1)}), bf16[384,1024]{1,0:T(8,128)(2,1)}) %reduce-scatter.2.cloned.1.call-update) | async-done | bytes 786448 | tf_op jit(solution)/shard_map/reduce_scatter | solution.py:136
  (701 shorter events, 375.7 us)
Async XLA Ops:
  6.5 39.9 %copy-start = (bf16[4096,256]{1,0:T(8,128)(2,1)S(1)}, bf16[4096,256]{1,0:T(8,128)(2,1)}, u32[]{:S(2)}) copy-start(bf16[4096,256]{1,0:T(8,128)(2,1)} %param.18) | copy-start | bytes 6291460
  6.5 39.9 %copy-start.4 = (f32[4096]{0:T(1024)S(1)}, f32[4096]{0:T(1024)}, u32[]{:S(2)}) copy-start(f32[4096]{0:T(1024)} %param.15) | copy-start | bytes 49156
  6.5 37.1 %all-gather.4.cloned.1.call-start = ((), (), s32[]{:S(2)}) async-start(), calls=%async_computation.1 | async-start | bytes 3932160 | tf_op jit(solution)/shard_map/all_gather | solution.py:38
  7.3 203.0 %all-gather.8.cloned.1.call-start = ((), (), s32[]{:S(2)}) async-start(), calls=%async_computation.3 | async-start | bytes 6488064 | tf_op jit(solution)/shard_map/all_gather | solution.py:65
  43.7 2.8 copy-start.2
  46.5 2.6 copy-start.1
  48.3 336.1 %all-gather.6.cloned.1.call-start = ((), (), s32[]{:S(2)}) async-start(), calls=%async_computation.2 | async-start | bytes 6488064 | tf_op jit(solution)/shard_map/all_gather | solution.py:64
  56.4 1793.1 %reduce-scatter.2.cloned.1.call-start = ((), (), s32[]{:S(2)}) async-start(), calls=%async_computation.4 | async-start | bytes 3932160 | tf_op jit(solution)/shard_map/reduce_scatter | solution.py:136
  1120.4 729.2 %copy-start.3 = (bf16[384,1024]{1,0:T(8,128)(2,1)S(1)}, bf16[384,1024]{1,0:T(8,128)(2,1)}, u32[]{:S(2)}) copy-start(bf16[384,1024]{1,0:T(8,128)(2,1)} %param.13) | copy-start | bytes 2359300
Sparse Core Ops, SparseCore 0:
  9.0 34.6 all-gather.3
  48.4 161.7 all-gather.7
  211.9 172.4 all-gather.5
  1120.6 728.9 reduce-scatter.1
where the time goes:
time: 1880 us; the launch traced here: 1860 us
  waiting for transfers between devices  1040 us (55%)
  loops' own time  382 us (20%)
  other arithmetic  242 us (13%)
  local copies, waits for them, and re-layouts  130 us (7%)
  matrix products  50.7 us (3%)
    reduce_scatter x1, waiting for transfers between devices, on_device(): lax.psum_scatter(products.astype(jnp.bfloat16), 'head', scatter_dimension...  729 us
    another operation x1, loops' own time, on_device(): lax.fori_loop(0, query_tiles * key_tiles, visit_tile, (zero_high, zero_de...  379 us
    all_gather x1, waiting for transfers between devices, on_device(): key_piece = lax.all_gather(keys_local, 'ctx', axis=0, tiled=True)  165 us
    reduce_max x144, other arithmetic, visit_tile(): jnp.max(key_spots) >= jnp.min(tile_starts)  111 us
    reduce_min x144, other arithmetic, visit_tile(): jnp.min(tile_starts)  110 us
    all_gather x1, waiting for transfers between devices, on_device(): value_piece = lax.all_gather(values_local, 'ctx', axis=0, tiled=True)  108 us
    dynamic_update_slice x16, local copies, waits for them, and re-layouts, update(): lax.dynamic_update_slice_in_dim(summed, new_summed, query_start, 2)  53.7 us
    gather x15, local copies, waits for them, and re-layouts, on_device(): starts = jnp.searchsorted(doc_ids, doc_ids[positions], side='left')  38 us
  transfers between devices with their start and end apart: 4, of which 4 were waited for; matrix products, arithmetic and copies ran while one was open for 3% of the time, Pallas kernels for 0%

commit v1 on v0

v1 whole, which is shorter than its diff:
```python
import functools
import math

import jax
import jax.numpy as jnp
import numpy as np
from jax import lax
from jax.experimental import pallas as pl
from jax.experimental.pallas import tpu as pltpu
from jax.sharding import PartitionSpec as P

MESH = pl.DeviceIdType.MESH
BF16 = jnp.bfloat16
F32 = jnp.float32
HD = 128
GROUP = 4
THETA = 500000.0
QR = 96
KB = 1024
VMEM_LIMIT = 60 * 2**20


def position():
    c, h = lax.axis_index("ctx"), lax.axis_index("head")
    return lax.div(h, 2), lax.rem(c, 2), lax.rem(lax.div(c, 2), 4), lax.div(c, 8), lax.rem(h, 2)


def device(xhi, xlo, y, z, core):
    return {"ctx": (z * 4 + y) * 2 + xlo, "head": xhi * 2 + core}


def wrap(v):
    return lax.rem(v + 4, 4)


def greet(peers):
    barrier = pltpu.get_barrier_semaphore()
    for peer in peers:
        pl.semaphore_signal(barrier, inc=1, device_id=peer, device_id_type=MESH)
    pl.semaphore_wait(barrier, len(peers))


def remote(src, dst, send, recv, peer):
    return pltpu.make_async_remote_copy(
        src_ref=src, dst_ref=dst, send_sem=send, recv_sem=recv, device_id=peer, device_id_type=MESH
    )


def rope_tables(rows, blocks):
    inverse = THETA ** (-np.arange(HD // 2, dtype=np.float64) / (HD // 2))
    near = np.arange(rows, dtype=np.float64)[:, None] * inverse[None, :]
    far = (np.arange(blocks, dtype=np.float64) * rows)[:, None] * inverse[None, :]

    def pair(a):
        return (
            np.concatenate([np.cos(a), np.cos(a)], 1).astype(np.float32),
            np.concatenate([np.sin(a), np.sin(a)], 1).astype(np.float32),
        )

    return pair(near) + pair(far)


def project_kernel(
    x_ref, gain_ref, cn_ref, sn_ref, cf_ref, sf_ref, wq_hbm, wk_hbm, wv_hbm,
    q_ref, kv_ref,
    xbuf, nbuf, wq, wk, wv, wsem, lsem, ssend, srecv, osend, orecv, fsend, frecv,
):
    xhi, xlo, y, z, core = position()
    head = xhi * 2 + core
    rows = x_ref.shape[0]
    nch = xbuf.shape[0]
    ch = rows // nch
    sib, opp = device(xhi, xlo, y, z, 1 - core), device(1 - xhi, xlo, y, z, core)
    hs, ho, hf = xhi * 2 + 1 - core, (1 - xhi) * 2 + core, (1 - xhi) * 2 + 1 - core
    loads = [
        pltpu.make_async_copy(a, b, wsem.at[i])
        for i, (a, b) in enumerate(((wk_hbm, wk), (wv_hbm, wv), (wq_hbm, wq)))
    ]
    greet([sib, opp])
    outs, sibs, owns = [], [], []
    for k in range(nch):
        src = x_ref.at[pl.ds(k * ch, ch)]
        outs.append(remote(src, xbuf.at[k, head], osend.at[k], orecv.at[k], opp))
        sibs.append(remote(src, xbuf.at[k, head], ssend.at[k], srecv.at[k], sib))
        owns.append(pltpu.make_async_copy(src, xbuf.at[k, head], lsem.at[k]))
        outs[k].start()
    for k in range(nch):
        sibs[k].start()
        owns[k].start()
    for load in loads:
        load.start()
    cn, sn = cn_ref[...], sn_ref[...]
    ctx = lax.axis_index("ctx")
    cf, sf = cf_ref[pl.ds(ctx, 1), :], sf_ref[pl.ds(ctx, 1), :]
    cos = cn * cf - sn * sf
    sin = sn * cf + cn * sf
    lane = lax.broadcasted_iota(jnp.int32, (rows, HD), 1)
    sin = jnp.where(lane < HD // 2, -sin, sin)

    def rope(v, k):
        lo = k * ch
        return v * cos[lo:lo + ch] + pltpu.roll(v, HD // 2, 1) * sin[lo:lo + ch]

    forwards = []
    for k in range(nch):
        remote(x_ref.at[pl.ds(k * ch, ch)], xbuf.at[k, ho], osend.at[k], orecv.at[k], opp).wait_recv()
        f = remote(xbuf.at[k, ho], xbuf.at[k, ho], fsend.at[k], frecv.at[k], sib)
        f.start()
        forwards.append(f)
        owns[k].wait()
        remote(x_ref.at[pl.ds(k * ch, ch)], xbuf.at[k, hs], ssend.at[k], srecv.at[k], sib).wait_recv()
        remote(xbuf.at[k, ho], xbuf.at[k, hf], fsend.at[k], frecv.at[k], sib).wait_recv()
        total = jnp.zeros((ch, 1), F32)
        width = x_ref.shape[1]
        for j in range(4):
            v = xbuf[k, j].astype(F32)
            total = total + jnp.sum(v * v, axis=1, keepdims=True)
        scale = lax.rsqrt(total / (4.0 * width) + 1e-05)
        for j in range(4):
            v = xbuf[k, j].astype(F32)
            nbuf[:, j * width:(j + 1) * width] = (
                v * scale * gain_ref[:, j * width:(j + 1) * width]
            ).astype(BF16)
        if k == 0:
            loads[0].wait()
            loads[1].wait()
        kk = jnp.dot(nbuf[...], wk[...], preferred_element_type=F32)
        vv = jnp.dot(nbuf[...], wv[...], preferred_element_type=F32)
        for hh in range(2):
            kv_ref[0, hh, k * ch:(k + 1) * ch, :] = rope(kk[:, hh * HD:(hh + 1) * HD], k).astype(BF16)
            kv_ref[1, hh, k * ch:(k + 1) * ch, :] = vv[:, hh * HD:(hh + 1) * HD].astype(BF16)
        if k == 0:
            loads[2].wait()
        for pairs in range(4):
            qq = jnp.dot(
                nbuf[...], wq[:, pairs * 256:(pairs + 1) * 256], preferred_element_type=F32
            )
            for u in range(2):
                g = (pairs % 2) * 2 + u
                out = rope(qq[:, u * HD:(u + 1) * HD], k).astype(BF16)
                for b in range(ch // QR):
                    gb = k * (ch // QR) + b
                    at = (gb // 2) * GROUP * QR + g * QR
                    q_ref[pairs // 2, gb % 2, at:at + QR, :] = out[b * QR:(b + 1) * QR]
    for k in range(nch):
        outs[k].wait_send()
        sibs[k].wait_send()
        forwards[k].wait_send()


def exchange_kernel(
    q_ref, kv_ref, qo_ref, kvo_ref,
    zsend, zrecv, qsend, qrecv, xsend, xrecv, ypsend, yprecv, ymsend, ymrecv, fsend, frecv, bsend, brecv,
):
    xhi, xlo, y, z, core = position()
    rows = kv_ref.shape[2]
    sib = device(xhi, xlo, y, z, 1 - core)
    side = device(xhi, 1 - xlo, y, z, core)
    up, down = device(xhi, xlo, wrap(y + 1), z, core), device(xhi, xlo, wrap(y - 1), z, core)
    ring = [device(xhi, xlo, y, wrap(z + d), c) for d in (1, 2, 3) for c in (0, 1)]
    greet(ring + [sib, side, up, down])

    def block(ref, comp, zz, yy, xx):
        return ref.at[comp, pl.ds(pl.multiple_of(((zz * 4 + yy) * 2 + xx) * rows, rows), rows)]

    def outgoing(hh, t, start):
        zt = 2 * core + hh
        slot = wrap(z - zt)
        i = hh * 2 + t
        pairs = (
            (kv_ref.at[t, hh], block(kvo_ref, t, z, y, xlo), zsend.at[i], zrecv.at[slot]),
            (q_ref.at[hh, t], qo_ref.at[z], qsend.at[i], qrecv.at[slot]),
        )
        here = jnp.logical_and(zt == z, core == t)

        for src, dst, ss, rs in pairs:
            @pl.when(here)
            def _():
                if start:
                    pltpu.make_async_copy(src, dst, rs).start()

            @pl.when(jnp.logical_not(here))
            def _():
                cp = remote(src, dst, ss, rs, device(xhi, xlo, y, zt, t))
                if start:
                    cp.start()
                else:
                    cp.wait_send()

    for hh in range(2):
        for t in range(2):
            outgoing(hh, t, True)

    sends = []

    def push(ref, ss, rs, peer):
        cp = remote(ref, ref, ss, rs, peer)
        cp.start()
        sends.append(cp)

    order = (0, 1, 3, 2)
    n = 0
    for i, d in enumerate(order):
        zz = wrap(z + d)
        ref = block(kvo_ref, core, zz, y, xlo)
        remote(kv_ref.at[0, 0], ref, zsend.at[0], zrecv.at[d], sib).wait_recv()
        push(ref, ypsend.at[i], yprecv.at[i], up)
        push(ref, ymsend.at[i], ymrecv.at[i], down)
        push(ref, xsend.at[i], xrecv.at[i], side)
        push(ref, bsend.at[n], brecv.at[n], sib)
        n += 1
    for i, d in enumerate(order):
        ref = block(kvo_ref, core, wrap(z + d), y, 1 - xlo)
        remote(ref, ref, xsend.at[i], xrecv.at[i], side).wait_recv()
        push(ref, ypsend.at[4 + i], yprecv.at[4 + i], up)
        push(ref, ymsend.at[4 + i], ymrecv.at[4 + i], down)
        push(ref, bsend.at[n], brecv.at[n], sib)
        n += 1
    for i in range(8):
        zz = wrap(z + order[i % 4])
        xx = xlo if i < 4 else 1 - xlo
        ref = block(kvo_ref, core, zz, wrap(y - 1), xx)
        remote(ref, ref, ypsend.at[i], yprecv.at[i], up).wait_recv()
        if i % 2 == 0:
            push(ref, fsend.at[i], frecv.at[i], up)
        push(ref, bsend.at[n], brecv.at[n], sib)
        n += 1
        ref = block(kvo_ref, core, zz, wrap(y + 1), xx)
        remote(ref, ref, ymsend.at[i], ymrecv.at[i], down).wait_recv()
        if i % 2 == 1:
            push(ref, fsend.at[i], frecv.at[i], down)
        push(ref, bsend.at[n], brecv.at[n], sib)
        n += 1
    for i in range(8):
        zz = wrap(z + order[i % 4])
        xx = xlo if i < 4 else 1 - xlo
        ref = block(kvo_ref, core, zz, wrap(y + 2), xx)
        remote(ref, ref, fsend.at[i], frecv.at[i], up).wait_recv()
        push(ref, bsend.at[n], brecv.at[n], sib)
        n += 1
    m = 0
    places = [(d, 0, 0) for d in order] + [(d, 0, 1) for d in order]
    for i in range(8):
        places += [(order[i % 4], 3, i // 4), (order[i % 4], 1, i // 4)]
    places += [(order[i % 4], 2, i // 4) for i in range(8)]
    for d, dy, other in places:
        xx = 1 - xlo if other else xlo
        ref = block(kvo_ref, 1 - core, wrap(z + d), wrap(y + dy), xx)
        remote(ref, ref, bsend.at[m], brecv.at[m], sib).wait_recv()
        m += 1
    for d in range(4):
        zz = wrap(z + d)
        remote(q_ref.at[0, 0], qo_ref.at[zz], qsend.at[0], qrecv.at[d], sib).wait_recv()
    for cp in sends:
        cp.wait_send()
    for hh in range(2):
        for t in range(2):
            outgoing(hh, t, False)


def attend_kernel(docs_ref, q_ref, k_ref, v_ref, o_ref, vt_ref):
    keys = k_ref.shape[0]
    m_rows = GROUP * QR
    tiles = q_ref.shape[0] // m_rows
    xhi, xlo, y, z, core = position()
    docs = docs_ref[...]
    b = [jnp.sum((docs < i).astype(jnp.int32)) for i in (1, 2, 3)]

    def start_of(p):
        return jnp.where(p >= b[2], b[2], jnp.where(p >= b[1], b[1], jnp.where(p >= b[0], b[0], 0)))

    tb = 512

    @pl.loop(0, keys // tb)
    def _(i):
        o = pl.multiple_of(i * tb, tb)
        vt_ref[:, pl.ds(o, tb)] = v_ref[pl.ds(o, tb), :].T

    c2 = (HD ** -0.5) * math.log2(math.e)
    per = tiles // 4
    plane = keys // 4
    block = plane // 8

    @pl.loop(0, tiles)
    def _(t):
        q0 = (
            lax.div(t, per) * plane + y * (2 * block) + xlo * block
            + (lax.rem(t, per) * 2 + core) * QR
        )
        q = q_ref[pl.ds(pl.multiple_of(t * m_rows, m_rows), m_rows), :]
        first, last = start_of(q0), start_of(q0 + QR - 1)
        t0 = first // KB
        t3 = (q0 + QR + KB - 1) // KB
        t1 = jnp.minimum((last + KB - 1) // KB, t3)
        t2 = jnp.maximum((q0 + 1) // KB, t1)
        qpos = q0 + lax.rem(lax.broadcasted_iota(jnp.int32, (1, m_rows), 1), QR)
        qst = start_of(qpos)

        def body(masked, i, carry):
            m, l, acc = carry
            o = pl.multiple_of(i * KB, KB)
            s = lax.dot_general(
                k_ref[pl.ds(o, KB), :], q, (((1,), (1,)), ((), ())), preferred_element_type=F32
            )
            if masked:
                kp = o + lax.broadcasted_iota(jnp.int32, (KB, m_rows), 0)
                s = jnp.where((kp <= qpos) & (kp >= qst), s, -1e30)
            mn = jnp.maximum(m, jnp.max(s, axis=0, keepdims=True))
            p = jnp.exp2((s - mn) * c2)
            a = jnp.exp2((m - mn) * c2)
            l = l * a + jnp.sum(p, axis=0, keepdims=True)
            acc = acc * a + jnp.dot(
                vt_ref[:, pl.ds(o, KB)], p.astype(BF16), preferred_element_type=F32
            )
            return mn, l, acc

        carry = (
            jnp.full((1, m_rows), -1e29, F32),
            jnp.zeros((1, m_rows), F32),
            jnp.zeros((HD, m_rows), F32),
        )
        carry = lax.fori_loop(t0, t1, functools.partial(body, True), carry)
        carry = lax.fori_loop(t1, t2, functools.partial(body, False), carry)
        m, l, acc = lax.fori_loop(t2, t3, functools.partial(body, True), carry)
        r = (acc / l).T.astype(BF16)
        ro = pl.multiple_of(t * QR, QR)
        for g in range(GROUP):
            o_ref[pl.ds(ro, QR), g * HD:(g + 1) * HD] = r[g * QR:(g + 1) * QR]


def output_kernel(
    att_ref, x_ref, w_hbm, o_ref,
    abuf, w, mine, theirs, part, recv_part, opp_part,
    wsem, asend, arecv, ssend, srecv, osend, orecv,
):
    xhi, xlo, y, z, core = position()
    sib, opp = device(xhi, xlo, y, z, 1 - core), device(1 - xhi, xlo, y, z, core)
    nj = att_ref.shape[1]
    width = x_ref.shape[1]
    owner = lax.div(z, 2)
    hz = lax.rem(z, 2)
    depth = w_hbm.shape[0]
    ncol = w_hbm.shape[1] // width
    loads = [
        pltpu.make_async_copy(
            w_hbm.at[:, pl.ds(pl.multiple_of(c * width, width), width)], w.at[i], wsem.at[i]
        )
        for i, c in enumerate(
            ((1 - xhi) * 2 + 1 - core, (1 - xhi) * 2 + core, xhi * 2 + 1 - core, xhi * 2 + core)
        )
    ]
    for load in loads:
        load.start()
    ring = [device(xhi, xlo, y, wrap(z + d), c) for d in (1, 2, 3) for c in (0, 1)]
    greet(ring + [sib, opp])

    def returning(d, j, start):
        zt = wrap(z + d)
        i = j * 4 + d
        src, dst = att_ref.at[zt, j], abuf.at[j, hz, core]
        slot = (j * 2 + hz) * 2 + core
        here = owner == core
        if d == 0:
            @pl.when(here)
            def _():
                if start:
                    pltpu.make_async_copy(src, dst, arecv.at[slot]).start()

            @pl.when(jnp.logical_not(here))
            def _():
                cp = remote(src, dst, asend.at[i], arecv.at[slot], sib)
                if start:
                    cp.start()
                else:
                    cp.wait_send()
        else:
            cp = remote(src, dst, asend.at[i], arecv.at[slot], device(xhi, xlo, y, zt, owner))
            if start:
                cp.start()
            else:
                cp.wait_send()

    for j in range(nj):
        for d in (1, 3, 2, 0):
            returning(d, j, True)
    waits = []
    opps = []
    for j in range(nj):
        for hh in range(2):
            for c in range(2):
                slot = (j * 2 + hh) * 2 + c
                remote(
                    att_ref.at[0, j], abuf.at[j, hh, c], asend.at[0], arecv.at[slot], sib
                ).wait_recv()

        def product(i):
            if j == 0:
                loads[i].wait()
            lhs = [
                jnp.concatenate([abuf[j, hh, 0], abuf[j, hh, 1]], axis=0) for hh in range(2)
            ]
            half = depth // 2
            return jnp.dot(lhs[0], w[i, :half], preferred_element_type=F32) + jnp.dot(
                lhs[1], w[i, half:], preferred_element_type=F32
            )

        for i in range(2):
            part[j, i] = product(2 * i).astype(BF16)
            cp = remote(part.at[j, i], recv_part.at[j, i], ssend.at[2 * j + i], srecv.at[2 * j + i], sib)
            cp.start()
            waits.append(cp)
            total = product(2 * i + 1)
            remote(
                part.at[j, i], recv_part.at[j, i], ssend.at[2 * j + i], srecv.at[2 * j + i], sib
            ).wait_recv()
            total = total + recv_part[j, i].astype(F32)
            if i == 0:
                theirs[j] = total.astype(BF16)
                cp = remote(theirs.at[j], opp_part.at[j], osend.at[j], orecv.at[j], opp)
                cp.start()
                opps.append(cp)
            else:
                mine[j] = total
    n = 2 * QR
    for j in range(nj):
        remote(theirs.at[j], opp_part.at[j], osend.at[j], orecv.at[j], opp).wait_recv()
        o_ref[j * n:(j + 1) * n, :] = (
            mine[j] + opp_part[j].astype(F32) + x_ref[j * n:(j + 1) * n, :].astype(F32)
        ).astype(BF16)
    for cp in waits + opps:
        cp.wait_send()
    for j in range(nj):
        for d in range(4):
            returning(d, j, False)


def vmem():
    return pl.BlockSpec(memory_space=pltpu.VMEM)


def hbm():
    return pl.BlockSpec(memory_space=pl.ANY)


def dma(n):
    return pltpu.SemaphoreType.DMA((n,))


def on_device(tables, tokens, doc_ids, norm_gain, w_query, w_key, w_value, w_out):
    rows, width = tokens.shape
    nch = 2
    ch = rows // nch
    keys = doc_ids.shape[0]
    blk = (rows // 2) * GROUP
    q, kv = pl.pallas_call(
        project_kernel,
        out_shape=(
            jax.ShapeDtypeStruct((2, 2, blk, HD), BF16),
            jax.ShapeDtypeStruct((2, 2, rows, HD), BF16),
        ),
        in_specs=[vmem()] * 6 + [hbm()] * 3,
        out_specs=(vmem(), vmem()),
        scratch_shapes=[
            pltpu.VMEM((nch, 4, ch, width), BF16),
            pltpu.VMEM((ch, 4 * width), BF16),
            pltpu.VMEM(w_query.shape, BF16),
            pltpu.VMEM(w_key.shape, BF16),
            pltpu.VMEM(w_value.shape, BF16),
            dma(3), dma(nch), dma(nch), dma(nch), dma(nch), dma(nch), dma(nch), dma(nch),
        ],
        compiler_params=pltpu.CompilerParams(
            collective_id=0, has_side_effects=True, vmem_limit_bytes=VMEM_LIMIT
        ),
        name="project",
    )(tokens, norm_gain.reshape(1, -1), *tables, w_query, w_key, w_value)
    q, kv = pl.pallas_call(
        exchange_kernel,
        out_shape=(
            jax.ShapeDtypeStruct((4, blk, HD), BF16),
            jax.ShapeDtypeStruct((2, keys, HD), BF16),
        ),
        in_specs=[hbm()] * 2,
        out_specs=(hbm(), hbm()),
        scratch_shapes=[
            dma(4), dma(4), dma(4), dma(4), dma(4), dma(4),
            dma(8), dma(8), dma(8), dma(8), dma(8), dma(8), dma(32), dma(32),
        ],
        compiler_params=pltpu.CompilerParams(collective_id=1, has_side_effects=True),
        name="exchange",
    )(q, kv)
    attended = pl.pallas_call(
        attend_kernel,
        out_shape=jax.ShapeDtypeStruct((4 * rows // 2, GROUP * HD), BF16),
        in_specs=[
            vmem(),
            vmem(),
            pl.BlockSpec((None, keys, HD), lambda i: (0, 0, 0)),
            pl.BlockSpec((None, keys, HD), lambda i: (1, 0, 0)),
        ],
        grid=(1,),
        out_specs=vmem(),
        scratch_shapes=[pltpu.VMEM((HD, keys), BF16)],
        compiler_params=pltpu.CompilerParams(vmem_limit_bytes=VMEM_LIMIT),
        name="attend",
    )(doc_ids.reshape(-1, 128), q.reshape(4 * blk, HD), kv, kv)
    nj = rows // (2 * QR)
    n = 2 * QR
    return pl.pallas_call(
        output_kernel,
        out_shape=jax.ShapeDtypeStruct((rows, width), BF16),
        in_specs=[hbm(), vmem(), hbm()],
        out_specs=vmem(),
        scratch_shapes=[
            pltpu.VMEM((nj, 2, 2, QR, GROUP * HD), BF16),
            pltpu.VMEM((4, w_out.shape[0], width), BF16),
            pltpu.VMEM((nj, n, width), F32),
            pltpu.VMEM((nj, n, width), BF16),
            pltpu.VMEM((nj, 2, n, width), BF16),
            pltpu.VMEM((nj, 2, n, width), BF16),
            pltpu.VMEM((nj, n, width), BF16),
            dma(4), dma(4 * nj), dma(4 * nj), dma(2 * nj), dma(2 * nj), dma(nj), dma(nj),
        ],
        compiler_params=pltpu.CompilerParams(
            collective_id=2, has_side_effects=True, vmem_limit_bytes=VMEM_LIMIT
        ),
        name="output",
    )(attended.reshape(4, nj, QR, GROUP * HD), tokens, w_out)


def solution(mesh):
    tables = rope_tables(384, mesh.shape["ctx"])

    def body(*args):
        return on_device(tuple(jnp.asarray(t) for t in tables), *args)

    in_specs = (
        P("ctx", "head"),
        P(),
        P(),
        P(None, "head"),
        P(None, "head"),
        P(None, "head"),
        P("head", None),
    )
    return jax.shard_map(
        body, mesh=mesh, in_specs=in_specs, out_specs=P("ctx", "head"), check_vma=False
    )
```

time: 1880 us -> 156 us (0.08); the launches traced: 1860 us -> 156 us
  waiting for transfers between devices: 1040 us -> 0 us
  loops' own time: 382 us -> 0 us
  other arithmetic: 242 us -> 0 us
  Pallas kernels: 0 us -> 154 us
  local copies, waits for them, and re-layouts: 130 us -> 2.06 us
  matrix products: 50.7 us -> 0 us
    reduce_scatter x1 -> x0, waiting for transfers between devices: 729 us -> none  [on_device(): lax.psum_scatter(products.astype(jnp.bfloat16), 'head', scatter_dimension...]
    another operation x146 -> x0, loops' own time: 382 us -> none  [the longest x1 379 us: on_device(): lax.fori_loop(0, query_tiles * key_tiles, visit_tile, (zero_high, zero_de...]
    all_gather x3 -> x0, waiting for transfers between devices: 310 us -> none  [the longest x1 165 us: on_device(): key_piece = lax.all_gather(keys_local, 'ctx', axis=0, tiled=True)]
    pallas_call x0 -> x4, Pallas kernels: none -> 154 us  [the longest x1 54.8 us: on_device(): pl.pallas_call(attend_kernel, out_shape=jax.ShapeDtypeStruct((4 * rows //...]
    reduce_max x144 -> x0, other arithmetic: 111 us -> none  [visit_tile(): jnp.max(key_spots) >= jnp.min(tile_starts)]
    reduce_min x144 -> x0, other arithmetic: 110 us -> none  [visit_tile(): jnp.min(tile_starts)]
    dynamic_update_slice x48 -> x0, local copies, waits for them, and re-layouts: 59.2 us -> none  [the longest x16 53.7 us: update(): lax.dynamic_update_slice_in_dim(summed, new_summed, query_start, 2)]
    dot_general x36 -> x0, matrix products: 50.7 us -> none  [the longest x16 22.8 us: update(): jnp.einsum('kgqj,jkd->kgqd', weights.astype(jnp.bfloat16), tile_values, p...]
  transfers between devices with their start and end apart: 4 -> 0, of which waited for: 4 -> 0; matrix products, arithmetic and copies ran while one was open for 3% -> 0% of each run, Pallas kernels for 0% -> 0%
where the time goes in v1:
time: 156 us
  Pallas kernels  154 us (99%)
  local copies, waits for them, and re-layouts  2.06 us (1%)
    pallas_call x1, Pallas kernels, on_device(): pl.pallas_call(attend_kernel, out_shape=jax.ShapeDtypeStruct((4 * rows //...  54.8 us
    pallas_call x1, Pallas kernels, on_device(): pl.pallas_call(exchange_kernel, out_shape=(jax.ShapeDtypeStruct((4, blk,...  38.3 us
    pallas_call x1, Pallas kernels, on_device(): pl.pallas_call(output_kernel, out_shape=jax.ShapeDtypeStruct((rows, width...  33.3 us
    pallas_call x1, Pallas kernels, on_device(): pl.pallas_call(project_kernel, out_shape=(jax.ShapeDtypeStruct((2, 2, blk...  27.4 us

profile of v1, /device:TPU:24, one launch (start us, length us, event | category | flops | bytes accessed | tf_op | source)
XLA Modules:
  0.0 155.9 jit_solution(6781946311027752099)
XLA Ops:
  0.0 27.4 %project.1 = (bf16[2,2,768,128]{3,2,1,0:T(8,128)(2,1)}, bf16[2,2,384,128]{3,2,1,0:T(8,128)(2,1)}) custom-call(bf16[384,1024]{1,0:T(8,128)(2,1)} %x_ref.3, f32[1,4096]{1,0:T(1,128)} %bitcast.7, f32[384,128]{1,0:T(8,128)} %constant.8.clone.cn_ref, f32[384,128]{1,0:T(8,128)} %constant.9.clone.sn_ref, f32[32,128]{1,0:T(8,128)} %constant.10.clone.cf_ref, ...), custom_call_target="tpu_custom_call" | custom-call | tf_op jit(solution)/shard_map/project/pallas_call | solution.py:455
  27.4 38.3 %exchange.1 = (bf16[4,768,128]{2,1,0:T(8,128)(2,1)}, bf16[2,12288,128]{2,1,0:T(8,128)(2,1)}) custom-call(bf16[2,2,768,128]{3,2,1,0:T(8,128)(2,1)} %get-tuple-element.9.q_ref, bf16[2,2,384,128]{3,2,1,0:T(8,128)(2,1)} %get-tuple-element.10.kv_ref), custom_call_target="tpu_custom_call" | custom-call | tf_op jit(solution)/shard_map/exchange/pallas_call | solution.py:476
  65.7 54.8 %attend.1 = bf16[768,512]{1,0:T(8,128)(2,1)} custom-call(s32[96,128]{1,0:T(8,128)} %bitcast.6, bf16[3072,128]{1,0:T(8,128)(2,1)} %bitcast.5, bf16[2,12288,128]{2,1,0:T(8,128)(2,1)} %get-tuple-element.12.k_ref.v_ref, bf16[2,12288,128]{2,1,0:T(8,128)(2,1)} %get-tuple-element.12.k_ref.v_ref), custom_call_target="tpu_custom_call" | custom-call | tf_op jit(solution)/shard_map/attend/pallas_call | solution.py:491
  120.5 33.3 %output.1 = bf16[384,1024]{1,0:T(8,128)(2,1)} custom-call(bf16[4,2,96,512]{3,2,1,0:T(8,128)(2,1)} %bitcast.4, bf16[384,1024]{1,0:T(8,128)(2,1)} %x_ref.3, bf16[1024,4096]{1,0:T(8,128)(2,1)} %w_hbm.1), custom_call_target="tpu_custom_call" | custom-call | tf_op jit(solution)/shard_map/output/pallas_call | solution.py:508
  153.8 2.1 %copy.13 = bf16[384,1024]{1,0:T(8,128)(2,1)} copy(bf16[384,1024]{1,0:T(8,128)(2,1)} %output.1) | data formatting | bytes 1572864
